TPU v7x, 128 devices: a whole 4x4x4 slice. The times are simulated.
128 devices in a mesh: dp: 8 (over x, core), ctx: 4 (over y), tensor: 4 (over z).
Axes of the slice: x: 4, y: 4, z: 4, core: 2. Of those that a mesh axis runs over, the one named last changes fastest.
Arguments:
- hidden: bfloat16 [8, 16384, 2560], P('dp', 'ctx', 'tensor'), may hold values from -6 to 6
- depth: int32 [8, 16384], P('dp', 'ctx'), may hold values from 1 to 4, as said below
- qkv_weight: bfloat16 [2560, 3, 2560], P(None, None, 'tensor'), may hold values from -0.125 to 0.125
- out_weight: bfloat16 [2560, 2560], P('tensor'), may hold values from -0.125 to 0.125
Outputs:
- update: bfloat16 [8, 16384, 2560], P('dp', 'ctx', 'tensor')
Inputs may be any that keep to these rules, and one draw needn't show every extreme that they name: In every aligned block of 4096 positions of a document at most 1024 tokens have depth at least 3, and some block has exactly 1024; over all documents exactly 16384 tokens do.
All inputs are finite; a program needn't handle non-finite values.
Results may differ from a plain program's by a relative error of at most 0.012.
The roundings to bfloat16 on the way count: a program that leaves them out, or rounds other values in their place, can miss the bound.
Values may be sent and summed in bfloat16 or wider, within the bound.
No kernel may reach another device: no remote copies, remote signals or barrier semaphores. Data moves between devices by JAX's collectives and lax.ppermute only.
A program may use at most 256 MiB of HBM per device.

v0:
```python
import jax
import jax.numpy as jnp
from jax import lax
from jax.sharding import PartitionSpec as P

HD = 128
RECURSION = 3
ACT_DEV = 512
CAP = 1024
score_scale = 0.25
norm_epsilon = 1e-05
head_epsilon = 1e-06


def head_normed(values):
    row_count = values.shape[0]
    per_head = values.reshape(row_count, -1, HD)
    factor = lax.rsqrt(jnp.mean(per_head * per_head, axis=2, keepdims=True) + head_epsilon)
    return (per_head * factor).reshape(row_count, -1).astype(jnp.bfloat16)


def project_rows(token_rows, qkv_weight):
    full_rows = lax.all_gather(token_rows, "tensor", axis=1, tiled=True)
    widened = full_rows.astype(jnp.float32)
    factor = lax.rsqrt(jnp.mean(widened * widened, axis=1, keepdims=True) + norm_epsilon)
    normed = (widened * factor).astype(jnp.bfloat16)
    head_width = qkv_weight.shape[2]
    projection = jnp.dot(
        normed,
        qkv_weight.reshape(qkv_weight.shape[0], 3 * head_width),
        preferred_element_type=jnp.float32,
    )
    queries = head_normed(projection[:, :head_width])
    keys_normed = head_normed(projection[:, head_width : 2 * head_width])
    values_out = projection[:, 2 * head_width :].astype(jnp.bfloat16)
    return jnp.concatenate([queries, keys_normed, values_out], axis=1)


def output_rows(context, out_weight):
    partial_value = jnp.dot(context, out_weight, preferred_element_type=jnp.float32)
    return lax.psum_scatter(
        partial_value.astype(jnp.bfloat16), "tensor", scatter_dimension=1, tiled=True
    )


def move_tiles(payload):
    return lax.all_to_all(payload, ("dp", "ctx"), split_axis=0, concat_axis=0, tiled=True)


def per_device(hidden, depth, qkv_weight, out_weight):
    tokens = hidden[0]
    local_len = tokens.shape[0]
    feature_width = tokens.shape[1]
    capacity = CAP
    head_width = out_weight.shape[0]
    heads_here = head_width // HD
    ctx_count = lax.axis_size("ctx")
    spread_size = lax.axis_size("dp") * ctx_count
    ctx_rank = lax.axis_index("ctx")
    my_index = lax.axis_index("dp") * ctx_count + ctx_rank
    active = (depth[0] >= RECURSION).astype(jnp.int32)
    active_count = jnp.sum(active)
    active_rank = jnp.cumsum(active) - 1
    slot_token = (
        jnp.zeros((capacity,), jnp.int32)
        .at[jnp.where(active > 0, active_rank, capacity)]
        .set(jnp.arange(local_len, dtype=jnp.int32), mode="drop")
    )
    filled = jnp.arange(capacity, dtype=jnp.int32) < active_count
    token_rows = jnp.where(filled[:, None], tokens[slot_token], jnp.zeros((), tokens.dtype))
    counts = lax.all_gather(active_count[None], ("dp", "ctx"), axis=0, tiled=True)
    doc_counts = lax.dynamic_slice_in_dim(counts, lax.axis_index("dp") * ctx_count, ctx_count)
    slot_size = capacity // spread_size
    offsets = jnp.cumsum(counts) - counts
    first_rank = offsets[my_index]
    global_rank = first_rank + jnp.arange(capacity, dtype=jnp.int32)
    target = global_rank % spread_size
    position = (
        global_rank // spread_size
        - first_rank // spread_size
        - (target < first_rank % spread_size).astype(jnp.int32)
    )
    send_at = jnp.where(filled, target * slot_size + position, capacity)
    fetch_at = jnp.minimum(send_at, capacity - 1)
    lower_bound = (offsets - my_index + spread_size - 1) // spread_size
    upper_bound = (offsets + counts - my_index + spread_size - 1) // spread_size
    arrived = (
        jnp.arange(slot_size, dtype=jnp.int32)[None, :] < (upper_bound - lower_bound)[:, None]
    ).reshape(-1)
    arrived_rank = jnp.cumsum(arrived.astype(jnp.int32)) - 1
    chosen = (
        jnp.zeros((ACT_DEV,), jnp.int32)
        .at[jnp.where(arrived, arrived_rank, ACT_DEV)]
        .set(jnp.arange(capacity, dtype=jnp.int32), mode="drop")
    )
    packed = (
        jnp.zeros((capacity,) + token_rows.shape[1:], token_rows.dtype)
        .at[send_at]
        .set(token_rows, mode="drop")
    )
    values = project_rows(move_tiles(packed)[chosen], qkv_weight)
    bring_packed = jnp.zeros((capacity,) + values.shape[1:], values.dtype).at[chosen].set(values)
    projected = move_tiles(bring_packed)[fetch_at]
    queries = projected[:, :head_width]
    key_values = projected[:, head_width:]
    query_heads = queries.reshape(capacity, heads_here, HD)
    key_piece = lax.all_gather(key_values, "ctx", axis=0, tiled=True)
    piece_rows = key_piece.shape[0]
    row_index = jnp.arange(piece_rows, dtype=jnp.int32)
    source_shard = row_index // capacity
    source_slot = row_index - source_shard * capacity
    clipped = jnp.clip(source_shard, 0, ctx_count - 1)
    key_filled = (source_shard >= 0) & (source_slot < doc_counts[clipped])
    same_block = (source_shard == ctx_rank)[None, :] & (
        slot_token[source_slot][None, :] <= slot_token[:, None]
    )
    earlier = (source_shard < ctx_rank)[None, :] | same_block
    allowed = earlier & key_filled[None, :] & filled[:, None]
    key_heads = key_piece[:, :head_width].reshape(piece_rows, heads_here, HD)
    value_heads = key_piece[:, head_width:].reshape(piece_rows, heads_here, HD)
    scores = (
        jnp.einsum("qhd,khd->hqk", query_heads, key_heads, preferred_element_type=jnp.float32)
        * score_scale
    )
    weights = jnp.where(allowed[None], jnp.exp(scores), 0.0)
    numerator = jnp.einsum(
        "hqk,khd->qhd",
        weights.astype(jnp.bfloat16),
        value_heads,
        preferred_element_type=jnp.float32,
    )
    denominator = jnp.sum(weights, axis=2)
    numerator, denominator = (numerator, denominator)
    guarded = denominator + (1.0 - filled.astype(jnp.float32))[None, :]
    context = (
        (numerator / jnp.transpose(guarded)[:, :, None])
        .reshape(capacity, head_width)
        .astype(jnp.bfloat16)
    )
    result_rows = output_rows(context, out_weight)
    update = (
        jnp.zeros((local_len, feature_width), jnp.bfloat16)
        .at[jnp.where(filled, slot_token, local_len)]
        .set(result_rows, mode="drop")
    )
    return update[None]


def solution(mesh):
    placed = (P("dp", "ctx", "tensor"), P("dp", "ctx"), P(None, None, "tensor"), P("tensor", None))
    return jax.shard_map(
        per_device, mesh=mesh, in_specs=placed, out_specs=P("dp", "ctx", "tensor"), check_vma=False
    )
```

profile of v0, /device:TPU:1, one launch (start us, length us, event | category | flops | bytes accessed | tf_op | source)
XLA Modules:
  0.0 554.3 jit_solution(16296913542401398679)
XLA Ops:
  6.5 0.9 compare_convert_fusion
  7.4 1.5 fusion.45
  9.0 1.2 dynamic-slice
  10.2 1.4 dynamic-update-slice
  11.6 16.9 %all-reduce = s32[32]{0:T(128)S(1)} all-reduce(s32[32]{0:T(128)S(1)} %dynamic-update-slice), channel_id=1, replica_groups=mesh['dp'=8,'ctx'=4,'tensor'=4] {'dp','ctx'}, use_global_device_ids=true, to_apply=%add | all-reduce | flops 32 | bytes 256
  28.5 0.1 copy.18
  28.6 0.1 reduce.2
  28.8 0.6 dynamic_slice.6
  31.9 0.6 iota_compare_fusion.1
  32.6 0.3 reduce-window.31
  33.0 0.1 slice_reduce_fusion
  33.2 0.8 compare_select_fusion.2
  33.9 15.5 %scatter_custom_fusion = s32[1024]{0:T(1024)S(1)} fusion(s32[4096]{0:T(1024)S(1)} %bitcast.67, s32[4096]{0:T(1024)S(1)} %iota.52, s32[]{:T(128)} %constant.133.clone.1), kind=kCustom, calls=%fused_computation.99 | custom fusion | bytes 4100 | tf_op jit(solution)/shard_map/scatter | solution.py:67
  49.5 1.2 fusion.34
  50.7 1.3 compare_select_fusion.6
  52.0 37.8 %scatter_custom_fusion.2 = bf16[1024,640]{1,0:T(8,128)(2,1)} fusion(s32[1024]{0:T(1024)S(1)} %bitcast.71, pred[1024]{0:T(1024)(128)(4,1)S(1)} %iota_compare_fusion.1, bf16[]{:T(256)} %constant.131.clone.1, bf16[4096,640]{1,0:T(8,128)(2,1)} %bitcast.59, s32[1024]{0:T(1024)S(1)} %get-tuple-element.13), kind=kCustom, calls=%fused_computation.37 | custom fusion | flops 655360 | bytes 6559744 | tf_op jit(solution)/shard_map/scatter | solution.py:99
  89.8 12.2 %all-to-all-start = ((bf16[32,32,640]{2,1,0:T(8,128)(2,1)}), bf16[32,32,640]{2,1,0:T(8,128)(2,1)}, u32[]{:S(2)}, u32[]{:S(2)}) async-start(bf16[32,32,640]{2,1,0:T(8,128)(2,1)} %bitcast.60), calls=%async_computation | async-start | bytes 2621440 | tf_op jit(solution)/shard_map/all_to_all | solution.py:47
  102.2 0.1 lt.196
  102.3 0.1 lt.202
  102.4 0.1 lt.198
  102.5 0.3 reduce-window.34
  102.9 0.1 slice_reduce_fusion.1
  103.1 4.8 scatter_custom_fusion.1
  107.9 13.0 %all-to-all-done = bf16[32,32,640]{2,1,0:T(8,128)(2,1)} async-done(((bf16[32,32,640]{2,1,0:T(8,128)(2,1)}), bf16[32,32,640]{2,1,0:T(8,128)(2,1)}, u32[]{:S(2)}, u32[]{:S(2)}) %all-to-all-start) | async-done | bytes 1310752 | tf_op jit(solution)/shard_map/all_to_all | solution.py:47
  120.9 4.3 gather_fusion
  125.2 13.9 %copy.19 = bf16[2560,3,640]{0,2,1:T(8,128)(2,1)} copy(bf16[2560,3,640]{2,0,1:T(8,128)(2,1)} %param.6) | data formatting | bytes 19660800 | tf_op args[2]
  139.1 21.1 %all-gather.6.cloned.1.call-done = bf16[512,2560]{1,0:T(8,128)(2,1)} async-done(((bf16[512,640]{1,0:T(8,128)(2,1)}), bf16[512,2560]{1,0:T(8,128)(2,1)}) %all-gather.6.cloned.1.call-update) | async-done | bytes 2621456 | tf_op jit(solution)/shard_map/all_gather | solution.py:23
  160.2 2.3 fusion.5
  162.5 9.3 %fusion.7 = f32[512,1920]{1,0:T(8,128)S(1)} fusion(bf16[2560,1920]{0,1:T(8,128)(2,1)} %bitcast.52, bf16[512,2560]{1,0:T(8,128)(2,1)} %all-gather.6.cloned.1.call-done, f32[512]{0:T(512)S(1)} %add_rsqrt_fusion.2), kind=kOutput, calls=%fused_computation.20 | convolution fusion | flops 5037096960 | bytes 16386048 | tf_op jit(solution)/shard_map/dot_general | solution.py:28
  171.8 1.0 slice.81
  172.8 1.2 copy-done.1
  174.0 1.7 slice_multiply_fusion.1
  175.7 2.8 copy.20
  178.5 1.4 reduce_sum.47
  179.9 1.2 mul.93
  181.2 2.8 copy.21
  183.9 2.8 copy.22
  186.8 1.4 reduce_sum.48
  188.2 1.2 mul.98
  189.5 2.8 copy.23
  192.3 3.8 multiply_convert_fusion.1
  196.1 7.0 %scatter_custom_fusion.3 = bf16[1024,1920]{1,0:T(8,128)(2,1)} fusion(s32[512]{0:T(512)S(1)} %compare_select_fusion.15, bf16[512,640]{1,0:T(8,128)(2,1)} %slice.81, bf16[]{:T(256)} %constant.171, bf16[512,640]{1,0:T(8,128)(2,1)} %get-tuple-element.10, bf16[512,640]{1,0:T(8,128)(2,1)} %get-tuple-element.9, bf16[]{:T(256)} %constant.131.clone.1), kind=kCustom, calls=%fused_computation.26 | custom fusion | flops 5898240 | bytes 5898244 | tf_op jit(solution)/shard_map/scatter | solution.py:102
  203.1 7.7 %all-to-all-start.1 = ((bf16[32,32,1920]{2,1,0:T(8,128)(2,1)}), bf16[32,32,1920]{2,1,0:T(8,128)(2,1)}, u32[]{:S(2)}, u32[]{:S(2)}) async-start(bf16[32,32,1920]{2,1,0:T(8,128)(2,1)} %bitcast.51), calls=%async_computation.1 | async-start | bytes 7864320 | tf_op jit(solution)/shard_map/all_to_all | solution.py:47
  210.9 47.3 %all-to-all-done.1 = bf16[32,32,1920]{2,1,0:T(8,128)(2,1)} async-done(((bf16[32,32,1920]{2,1,0:T(8,128)(2,1)}), bf16[32,32,1920]{2,1,0:T(8,128)(2,1)}, u32[]{:S(2)}, u32[]{:S(2)}) %all-to-all-start.1) | async-done | bytes 3932192 | tf_op jit(solution)/shard_map/all_to_all | solution.py:47
  258.2 11.1 %gather_fusion.1 = bf16[1024,1920]{1,0:T(8,128)(2,1)} fusion(bf16[1024,1920]{1,0:T(8,128)(2,1)} %bitcast.20, s32[1024]{0:T(1024)S(1)} %broadcast_clamp_fusion.1), kind=kCustom, calls=%fused_computation.2 | custom fusion | bytes 7868416 | tf_op jit(solution)/shard_map/gather | solution.py:103
  269.3 3.4 slice.66
  272.8 16.7 %gather_fusion.2 = s32[4096]{0:T(1024)S(1)} fusion(s32[1024]{0:T(1024)S(1)} %scatter_custom_fusion, s32[4096]{0:T(1024)S(1)} %broadcast_clamp_fusion), kind=kCustom, calls=%fused_computation.3 | custom fusion | bytes 49152 | tf_op jit(solution)/shard_map/gather | solution.py:115
  289.6 0.6 convert_subtract_fusion
  290.3 0.6 fusion.47
  290.9 2.4 compare_select_fusion.3
  293.3 6.2 %and_and_fusion = pred[1024,4096]{1,0:T(8,128)(4,1)} fusion(s32[4096]{0:T(1024)S(1)} %gather_fusion.2, s32[1024]{0:T(1024)S(1)} %scatter_custom_fusion, pred[1024]{0:T(1024)(128)(4,1)S(1)} %iota_compare_fusion.1, pred[4096]{0:T(1024)(128)(4,1)S(1)} %fusion.32, pred[4096]{0:T(1024)(128)(4,1)S(1)} %get-tuple-element.23, pred[4096]{0:T(1024)(128)(4,1)S(1)} %get-tuple-element.24), kind=kLoop, calls=%fused_computation.14 | loop fusion | flops 20971520 | bytes 4228096 | tf_op jit(solution)/shard_map/and | solution.py:118
  299.5 2.5 slice.68
  302.1 2.5 copy.25
  304.5 69.3 %all-gather.4.cloned.1.call-done = bf16[4096,1280]{1,0:T(8,128)(2,1)} async-done(((bf16[1024,1280]{1,0:T(8,128)(2,1)}), bf16[4096,1280]{1,0:T(8,128)(2,1)}) %all-gather.4.cloned.1.call-update) | async-done | bytes 10485776 | tf_op jit(solution)/shard_map/all_gather | solution.py:107
  373.8 9.0 %fusion.46 = (bf16[4096,640]{1,0:T(8,128)(2,1)}, bf16[4096,640]{1,0:T(8,128)(2,1)}) fusion(bf16[4096,1280]{1,0:T(8,128)(2,1)} %all-gather.4.cloned.1.call-done), kind=kLoop, calls=%fused_computation.116 | loop fusion | bytes 20971520 | tf_op jit(solution)/shard_map/slice | solution.py:119
  382.8 7.9 %copy.24 = bf16[4096,640]{0,1:T(8,128)(2,1)} copy(bf16[4096,640]{1,0:T(8,128)(2,1)} %get-tuple-element.8) | data formatting | bytes 10485760 | tf_op jit(solution)/shard_map/slice | solution.py:120
  390.8 8.0 %copy.26 = bf16[4096,640]{0,1:T(8,128)(2,1)} copy(bf16[4096,640]{1,0:T(8,128)(2,1)} %get-tuple-element.7) | data formatting | bytes 10485760 | tf_op jit(solution)/shard_map/slice | solution.py:119
  398.8 36.3 %fusion = (f32[5,1024]{1,0:T(8,128)S(1)}, f32[5,1024,4096]{2,1,0:T(8,128)}) fusion(pred[1024,4096]{1,0:T(8,128)(4,1)} %and_and_fusion, bf16[1024,5,128]{0,2,1:T(8,128)(2,1)} %bitcast.61, bf16[4096,5,128]{0,2,1:T(8,128)(2,1)} %bitcast.54), kind=kOutput, calls=%fused_computation.10 | convolution fusion | flops 5431618560 | bytes 94654464 | tf_op jit(solution)/shard_map/qhd,khd->hqk/dot_general | solution.py:122
  435.1 30.0 %fusion.9 = bf16[1024,5,128]{0,2,1:T(8,128)(2,1)S(1)} fusion(bf16[4096,5,128]{0,2,1:T(8,128)(2,1)} %bitcast.53, f32[5,1024,4096]{2,1,0:T(8,128)} %get-tuple-element.20, pred[1024,4096]{1,0:T(8,128)(4,1)} %and_and_fusion, f32[1024,5]{0,1:T(8,128)S(1)} %add_bitcast_fusion), kind=kOutput, calls=%fused_computation.22 | convolution fusion | flops 5432934400 | bytes 94654464 | tf_op jit(solution)/shard_map/hqk,khd->qhd/dot_general | solution.py:126
  465.1 6.3 %convolution_convert_fusion = bf16[1024,2560]{1,0:T(8,128)(2,1)} fusion(bf16[1024,640]{0,1:T(8,128)(2,1)S(1)} %bitcast.73, bf16[640,2560]{1,0:T(8,128)(2,1)S(1)} %copy-done), kind=kOutput, calls=%fused_computation.17 | convolution fusion | flops 3358064640 | bytes 9830400 | tf_op jit(solution)/shard_map/dot_general | solution.py:40
  471.4 8.0 %copy.31 = bf16[1024,2560]{0,1:T(8,128)(2,1)} copy(bf16[1024,2560]{1,0:T(8,128)(2,1)} %convolution_convert_fusion) | data formatting | bytes 10485760
  479.4 56.8 %reduce-scatter.4.cloned.1.call-done = bf16[640,1024]{1,0:T(8,128)(2,1)} async-done(((bf16[2560,1024]{1,0:T(8,128)(2,1)}), bf16[640,1024]{1,0:T(8,128)(2,1)}) %reduce-scatter.4.cloned.1.call-update) | async-done | bytes 1310736
  536.2 2.4 copy.32
  538.6 9.0 %scatter_custom_fusion.4 = bf16[4096,640]{1,0:T(8,128)(2,1)} fusion(s32[1024]{0:T(1024)} %get-tuple-element.14, bf16[1024,640]{1,0:T(8,128)(2,1)} %copy.32, bf16[]{:T(256)} %constant.131.clone.1), kind=kCustom, calls=%fused_computation.24 | custom fusion | bytes 5243392 | tf_op jit(solution)/shard_map/scatter | solution.py:144
  (38 shorter events, 1.1 us)
Async XLA Ops:
  6.5 458.6 %copy-start = (bf16[640,2560]{1,0:T(8,128)(2,1)S(1)}, bf16[640,2560]{1,0:T(8,128)(2,1)}, u32[]{:S(2)}) copy-start(bf16[640,2560]{1,0:T(8,128)(2,1)} %param.7) | copy-start | bytes 9830404
  89.8 31.1 %all-to-all-start = ((bf16[32,32,640]{2,1,0:T(8,128)(2,1)}), bf16[32,32,640]{2,1,0:T(8,128)(2,1)}, u32[]{:S(2)}, u32[]{:S(2)}) async-start(bf16[32,32,640]{2,1,0:T(8,128)(2,1)} %bitcast.60), calls=%async_computation | async-start | bytes 2621440 | tf_op jit(solution)/shard_map/all_to_all | solution.py:47
  102.0 58.2 %all-gather.6.cloned.1.call-start = ((), (), s32[]{:S(2)}) async-start(), calls=%async_computation.4 | async-start | bytes 3276800 | tf_op jit(solution)/shard_map/all_gather | solution.py:23
  171.8 2.1 copy-start.1
  203.1 55.1 %all-to-all-start.1 = ((bf16[32,32,1920]{2,1,0:T(8,128)(2,1)}), bf16[32,32,1920]{2,1,0:T(8,128)(2,1)}, u32[]{:S(2)}, u32[]{:S(2)}) async-start(bf16[32,32,1920]{2,1,0:T(8,128)(2,1)} %bitcast.51), calls=%async_computation.1 | async-start | bytes 7864320 | tf_op jit(solution)/shard_map/all_to_all | solution.py:47
  210.8 163.0 %all-gather.4.cloned.1.call-start = ((), (), s32[]{:S(2)}) async-start(), calls=%async_computation.3 | async-start | bytes 13107200 | tf_op jit(solution)/shard_map/all_gather | solution.py:107
  272.7 263.4 %reduce-scatter.4.cloned.1.call-start = ((), (), s32[]{:S(2)}) async-start(), calls=%async_computation.5 | async-start | bytes 6553600
Sparse Core Ops, SparseCore 0:
  125.4 34.7 all-gather.5
  272.9 100.8 all-gather.3
  479.5 56.6 reduce-scatter.3
where the time goes:
time: 563 us; the launch traced here: 554 us
  waiting for transfers between devices  208 us (37%)
  local copies, waits for them, and re-layouts  140 us (25%)
  matrix products  81.8 us (15%)
  other arithmetic  72.3 us (13%)
  starting transfers between devices  20 us (4%)
  blocking collectives  16.9 us (3%)
  between operations  16.2 us (3%)
    all_gather x1, waiting for transfers between devices, per_device(): key_piece = lax.all_gather(key_values, 'ctx', axis=0, tiled=True)  69.3 us
    all_to_all x2, waiting for transfers between devices, move_tiles(): lax.all_to_all(payload, ('dp', 'ctx'), split_axis=0, concat_axis=0, tiled...  60.3 us
    unnamed x4, waiting for transfers between devices  56.9 us
    scatter x1, other arithmetic, per_device(): packed = jnp.zeros((capacity,) + token_rows.shape[1:], token_rows.dtype)....  37.8 us
    dot_general x1, matrix products, per_device(): jnp.einsum('qhd,khd->hqk', query_heads, key_heads, preferred_element_type...  36.3 us
    dot_general x1, matrix products, per_device(): jnp.einsum('hqk,khd->qhd', weights.astype(jnp.bfloat16), value_heads, pre...  30 us
    unnamed x10, local copies, waits for them, and re-layouts  28 us
    all_gather x1, waiting for transfers between devices, project_rows(): full_rows = lax.all_gather(token_rows, 'tensor', axis=1, tiled=True)  21.1 us
  transfers between devices with their start and end apart: 5, of which 5 were waited for; matrix products, arithmetic and copies ran while one was open for 9% of the time, Pallas kernels for 0%

commit v1 on v0

--- a/solution.py
+++ b/solution.py
@@ -104,7 +104,8 @@
     queries = projected[:, :head_width]
     key_values = projected[:, head_width:]
     query_heads = queries.reshape(capacity, heads_here, HD)
-    key_piece = lax.all_gather(key_values, "ctx", axis=0, tiled=True)
+    sent = jnp.stack([key_values] * lax.axis_size("ctx"))
+    key_piece = jnp.concatenate(lax.all_to_all(sent, "ctx", 0, 0), axis=0)
     piece_rows = key_piece.shape[0]
     row_index = jnp.arange(piece_rows, dtype=jnp.int32)
     source_shard = row_index // capacity

time: 563 us -> 588 us (1.044)
  waiting for transfers between devices: 208 us -> 220 us
  local copies, waits for them, and re-layouts: 140 us -> 146 us
  starting transfers between devices: 20 us -> 26 us
    all_to_all x0 -> x1, waiting for transfers between devices: none -> 83.1 us  [per_device(): key_piece = jnp.concatenate(lax.all_to_all(sent, 'ctx', 0, 0), axis=0)]
    all_gather x1 -> x0, waiting for transfers between devices: 69.3 us -> none  [per_device(): key_piece = lax.all_gather(key_values, 'ctx', axis=0, tiled=True)]
    reshape x0 -> x1, local copies, waits for them, and re-layouts: none -> 9.67 us  [per_device(): key_piece = jnp.concatenate(lax.all_to_all(sent, 'ctx', 0, 0), axis=0)]
    slice x2 -> x1, local copies, waits for them, and re-layouts: 8.02 us -> 0.08 us  [the longest x1 7.94 us: per_device(): value_heads = key_piece[:, head_width:].reshape(piece_rows, heads_here, HD)]
    slice x2 -> x1, local copies, waits for them, and re-layouts: 17.1 us -> 9.78 us  [per_device(): key_heads = key_piece[:, :head_width].reshape(piece_rows, heads_here, HD)]
    another operation x4 -> x5, local copies, waits for them, and re-layouts: 0.39 us -> 7.5 us  [the longest x1 7.11 us: per_device(): sent = jnp.stack([key_values] * lax.axis_size('ctx'))]
    all_to_all x0 -> x1, starting transfers between devices: none -> 5.99 us  [per_device(): key_piece = jnp.concatenate(lax.all_to_all(sent, 'ctx', 0, 0), axis=0)]
    unnamed x4 -> x3, waiting for transfers between devices: 56.9 us -> 55.1 us
where the time goes in v1:
time: 588 us; the launch traced here: 579 us
  waiting for transfers between devices  220 us (37%)
  local copies, waits for them, and re-layouts  146 us (25%)
  matrix products  82.1 us (14%)
  other arithmetic  72.3 us (12%)
  starting transfers between devices  26 us (4%)
  blocking collectives  16.9 us (3%)
  between operations  16.5 us (3%)
    all_to_all x1, waiting for transfers between devices, per_device(): key_piece = jnp.concatenate(lax.all_to_all(sent, 'ctx', 0, 0), axis=0)  83.1 us
    all_to_all x2, waiting for transfers between devices, move_tiles(): lax.all_to_all(payload, ('dp', 'ctx'), split_axis=0, concat_axis=0, tiled...  60.4 us
    unnamed x3, waiting for transfers between devices  55.1 us
    scatter x1, other arithmetic, per_device(): packed = jnp.zeros((capacity,) + token_rows.shape[1:], token_rows.dtype)....  37.8 us
    dot_general x1, matrix products, per_device(): jnp.einsum('qhd,khd->hqk', query_heads, key_heads, preferred_element_type...  36.3 us
    dot_general x1, matrix products, per_device(): jnp.einsum('hqk,khd->qhd', weights.astype(jnp.bfloat16), value_heads, pre...  30.4 us
    unnamed x10, local copies, waits for them, and re-layouts  28 us
    all_gather x1, waiting for transfers between devices, project_rows(): full_rows = lax.all_gather(token_rows, 'tensor', axis=1, tiled=True)  21.1 us
  transfers between devices with their start and end apart: 5, of which 5 were waited for; matrix products, arithmetic and copies ran while one was open for 9% of the time, Pallas kernels for 0%

profile of v1, /device:TPU:1, one launch (start us, length us, event | category | flops | bytes accessed | tf_op | source)
XLA Modules:
  0.0 579.2 jit_solution(11722300226851773190)
XLA Ops:
  6.5 0.9 compare_convert_fusion
  7.4 1.5 fusion.45
  9.0 1.2 dynamic-slice
  10.2 1.4 dynamic-update-slice
  11.6 16.9 %all-reduce = s32[32]{0:T(128)S(1)} all-reduce(s32[32]{0:T(128)S(1)} %dynamic-update-slice), channel_id=1, replica_groups=mesh['dp'=8,'ctx'=4,'tensor'=4] {'dp','ctx'}, use_global_device_ids=true, to_apply=%add | all-reduce | flops 32 | bytes 256
  28.5 0.1 copy.17
  28.6 0.1 reduce.2
  28.8 0.6 dynamic_slice.6
  31.9 0.6 iota_compare_fusion.1
  32.6 0.3 reduce-window.31
  33.0 0.1 slice_reduce_fusion
  33.2 0.8 compare_select_fusion.2
  33.9 15.5 %scatter_custom_fusion = s32[1024]{0:T(1024)S(1)} fusion(s32[4096]{0:T(1024)S(1)} %bitcast.70, s32[4096]{0:T(1024)S(1)} %iota.52, s32[]{:T(128)} %constant.133.clone.1), kind=kCustom, calls=%fused_computation.99 | custom fusion | bytes 4100 | tf_op jit(solution)/shard_map/scatter | solution.py:67
  49.5 1.2 fusion.34
  50.7 1.3 compare_select_fusion.6
  52.0 37.8 %scatter_custom_fusion.2 = bf16[1024,640]{1,0:T(8,128)(2,1)} fusion(s32[1024]{0:T(1024)S(1)} %bitcast.74, pred[1024]{0:T(1024)(128)(4,1)S(1)} %iota_compare_fusion.1, bf16[]{:T(256)} %constant.131.clone.1, bf16[4096,640]{1,0:T(8,128)(2,1)} %bitcast.62, s32[1024]{0:T(1024)S(1)} %get-tuple-element.13), kind=kCustom, calls=%fused_computation.37 | custom fusion | flops 655360 | bytes 6559744 | tf_op jit(solution)/shard_map/scatter | solution.py:99
  89.8 12.2 %all-to-all-start = ((bf16[32,32,640]{2,1,0:T(8,128)(2,1)}), bf16[32,32,640]{2,1,0:T(8,128)(2,1)}, u32[]{:S(2)}, u32[]{:S(2)}) async-start(bf16[32,32,640]{2,1,0:T(8,128)(2,1)} %bitcast.63), calls=%async_computation | async-start | bytes 2621440 | tf_op jit(solution)/shard_map/all_to_all | solution.py:47
  102.2 0.1 lt.196
  102.5 0.3 reduce-window.34
  102.9 0.1 slice_reduce_fusion.1
  103.1 4.8 scatter_custom_fusion.1
  107.9 13.0 %all-to-all-done = bf16[32,32,640]{2,1,0:T(8,128)(2,1)} async-done(((bf16[32,32,640]{2,1,0:T(8,128)(2,1)}), bf16[32,32,640]{2,1,0:T(8,128)(2,1)}, u32[]{:S(2)}, u32[]{:S(2)}) %all-to-all-start) | async-done | bytes 1310752 | tf_op jit(solution)/shard_map/all_to_all | solution.py:47
  120.9 4.3 gather_fusion
  125.3 13.9 %copy.18 = bf16[2560,3,640]{0,2,1:T(8,128)(2,1)} copy(bf16[2560,3,640]{2,0,1:T(8,128)(2,1)} %param.6) | data formatting | bytes 19660800 | tf_op args[2]
  139.1 21.1 %all-gather.3.cloned.1.call-done = bf16[512,2560]{1,0:T(8,128)(2,1)} async-done(((bf16[512,640]{1,0:T(8,128)(2,1)}), bf16[512,2560]{1,0:T(8,128)(2,1)}) %all-gather.3.cloned.1.call-update) | async-done | bytes 2621456 | tf_op jit(solution)/shard_map/all_gather | solution.py:23
  160.2 2.3 fusion.5
  162.6 9.2 %fusion.7 = f32[512,1920]{1,0:T(8,128)S(1)} fusion(bf16[2560,1920]{0,1:T(8,128)(2,1)} %bitcast.55, bf16[512,2560]{1,0:T(8,128)(2,1)} %all-gather.3.cloned.1.call-done, f32[512]{0:T(512)S(1)} %add_rsqrt_fusion.2), kind=kOutput, calls=%fused_computation.20 | convolution fusion | flops 5037096960 | bytes 16386048 | tf_op jit(solution)/shard_map/dot_general | solution.py:28
  171.8 1.0 slice.81
  172.8 1.1 copy-done.1
  173.9 1.7 slice_multiply_fusion.1
  175.6 2.8 copy.19
  178.4 1.4 reduce_sum.47
  179.9 1.2 mul.93
  181.1 2.8 copy.20
  183.9 2.8 copy.21
  186.7 1.4 reduce_sum.48
  188.2 1.2 mul.98
  189.4 2.8 copy.22
  192.2 3.8 multiply_convert_fusion.1
  196.0 7.0 %scatter_custom_fusion.3 = bf16[1024,1920]{1,0:T(8,128)(2,1)} fusion(s32[512]{0:T(512)S(1)} %compare_select_fusion.15, bf16[512,640]{1,0:T(8,128)(2,1)} %slice.81, bf16[]{:T(256)} %constant.171, bf16[512,640]{1,0:T(8,128)(2,1)} %get-tuple-element.10, bf16[512,640]{1,0:T(8,128)(2,1)} %get-tuple-element.9, bf16[]{:T(256)} %constant.131.clone.1), kind=kCustom, calls=%fused_computation.26 | custom fusion | flops 5898240 | bytes 5898244 | tf_op jit(solution)/shard_map/scatter | solution.py:102
  203.0 7.7 %all-to-all-start.1 = ((bf16[32,32,1920]{2,1,0:T(8,128)(2,1)}), bf16[32,32,1920]{2,1,0:T(8,128)(2,1)}, u32[]{:S(2)}, u32[]{:S(2)}) async-start(bf16[32,32,1920]{2,1,0:T(8,128)(2,1)} %bitcast.54), calls=%async_computation.1 | async-start | bytes 7864320 | tf_op jit(solution)/shard_map/all_to_all | solution.py:47
  210.8 47.4 %all-to-all-done.1 = bf16[32,32,1920]{2,1,0:T(8,128)(2,1)} async-done(((bf16[32,32,1920]{2,1,0:T(8,128)(2,1)}), bf16[32,32,1920]{2,1,0:T(8,128)(2,1)}, u32[]{:S(2)}, u32[]{:S(2)}) %all-to-all-start.1) | async-done | bytes 3932192 | tf_op jit(solution)/shard_map/all_to_all | solution.py:47
  258.2 11.1 %gather_fusion.1 = bf16[1024,1920]{1,0:T(8,128)(2,1)} fusion(bf16[1024,1920]{1,0:T(8,128)(2,1)} %bitcast.20, s32[1024]{0:T(1024)S(1)} %broadcast_clamp_fusion.1), kind=kCustom, calls=%fused_computation.2 | custom fusion | bytes 7868416 | tf_op jit(solution)/shard_map/gather | solution.py:103
  269.2 3.4 slice.66
  272.7 4.5 copy.23
  277.2 7.1 %stack.2 = bf16[4,1024,1280]{1,2,0:T(8,128)(2,1)} broadcast(bf16[1024,1280]{0,1:T(8,128)(2,1)} %copy.23), dimensions={1,2} | broadcast | bytes 13107200 | tf_op jit(solution)/shard_map/stack | solution.py:107
  284.3 6.0 %all-to-all-start.2 = ((bf16[4,1024,1280]{1,2,0:T(8,128)(2,1)}), bf16[4,1024,1280]{1,2,0:T(8,128)(2,1)}, u32[]{:S(2)}, u32[]{:S(2)}) async-start(bf16[4,1024,1280]{1,2,0:T(8,128)(2,1)} %stack.2), calls=%async_computation.2 | async-start | bytes 20971520 | tf_op jit(solution)/shard_map/all_to_all | solution.py:108
  290.4 16.7 %gather_fusion.2 = s32[4096]{0:T(1024)S(1)} fusion(s32[1024]{0:T(1024)S(1)} %scatter_custom_fusion, s32[4096]{0:T(1024)S(1)} %broadcast_clamp_fusion), kind=kCustom, calls=%fused_computation.3 | custom fusion | bytes 49152 | tf_op jit(solution)/shard_map/gather | solution.py:116
  307.2 0.6 convert_subtract_fusion
  307.8 0.7 fusion.47
  308.5 2.5 compare_select_fusion.3
  311.0 6.3 %and_and_fusion = pred[1024,4096]{1,0:T(8,128)(4,1)} fusion(s32[4096]{0:T(1024)S(1)} %gather_fusion.2, s32[1024]{0:T(1024)S(1)} %scatter_custom_fusion, pred[1024]{0:T(1024)(128)(4,1)S(1)} %iota_compare_fusion.1, pred[4096]{0:T(1024)(128)(4,1)S(1)} %fusion.32, pred[4096]{0:T(1024)(128)(4,1)S(1)} %get-tuple-element.23, pred[4096]{0:T(1024)(128)(4,1)S(1)} %get-tuple-element.24), kind=kLoop, calls=%fused_computation.14 | loop fusion | flops 20971520 | bytes 4228096 | tf_op jit(solution)/shard_map/and | solution.py:119
  317.3 2.5 slice.68
  319.8 2.5 copy.25
  322.3 83.1 %all-to-all-done.2 = bf16[4,1024,1280]{1,2,0:T(8,128)(2,1)} async-done(((bf16[4,1024,1280]{1,2,0:T(8,128)(2,1)}), bf16[4,1024,1280]{1,2,0:T(8,128)(2,1)}, u32[]{:S(2)}, u32[]{:S(2)}) %all-to-all-start.2) | async-done | bytes 10485792 | tf_op jit(solution)/shard_map/all_to_all | solution.py:108
  405.3 9.7 %copy.32 = bf16[4,160,8,1024]{3,2,0,1:T(8,128)(2,1)} copy(bf16[4,160,8,1024]{3,2,1,0:T(8,128)(2,1)} %bitcast.37) | data formatting | bytes 20971520 | tf_op jit(solution)/shard_map/reshape | solution.py:108
  415.0 9.8 %fusion.46 = (bf16[4096,640]{0,1:T(8,128)(2,1)}, bf16[4096,640]{0,1:T(8,128)(2,1)}) fusion(bf16[4096,1280]{0,1:T(8,128)(2,1)} %bitcast.52), kind=kLoop, calls=%fused_computation.116 | loop fusion | bytes 20971520 | tf_op jit(solution)/shard_map/slice | solution.py:120
  424.8 36.3 %fusion = (f32[5,1024]{1,0:T(8,128)S(1)}, f32[5,1024,4096]{2,1,0:T(8,128)}) fusion(pred[1024,4096]{1,0:T(8,128)(4,1)} %and_and_fusion, bf16[1024,5,128]{0,2,1:T(8,128)(2,1)} %bitcast.64, bf16[4096,5,128]{0,2,1:T(8,128)(2,1)} %bitcast.57), kind=kOutput, calls=%fused_computation.10 | convolution fusion | flops 5431618560 | bytes 94654464 | tf_op jit(solution)/shard_map/qhd,khd->hqk/dot_general | solution.py:123
  461.1 30.4 %fusion.9 = bf16[1024,5,128]{0,2,1:T(8,128)(2,1)S(1)} fusion(bf16[4096,5,128]{0,2,1:T(8,128)(2,1)} %bitcast.56, f32[5,1024,4096]{2,1,0:T(8,128)} %get-tuple-element.20, pred[1024,4096]{1,0:T(8,128)(4,1)} %and_and_fusion, f32[1024,5]{0,1:T(8,128)S(1)} %add_bitcast_fusion), kind=kOutput, calls=%fused_computation.22 | convolution fusion | flops 5432934400 | bytes 94654464 | tf_op jit(solution)/shard_map/hqk,khd->qhd/dot_general | solution.py:127
  491.5 6.1 %convolution_convert_fusion = bf16[1024,2560]{1,0:T(8,128)(2,1)} fusion(bf16[1024,640]{0,1:T(8,128)(2,1)S(1)} %bitcast.76, bf16[640,2560]{1,0:T(8,128)(2,1)S(1)} %copy-done), kind=kOutput, calls=%fused_computation.17 | convolution fusion | flops 3358064640 | bytes 9830400 | tf_op jit(solution)/shard_map/dot_general | solution.py:40
  497.6 8.0 %copy.30 = bf16[1024,2560]{0,1:T(8,128)(2,1)} copy(bf16[1024,2560]{1,0:T(8,128)(2,1)} %convolution_convert_fusion) | data formatting | bytes 10485760
  505.6 55.1 %reduce-scatter.4.cloned.1.call-done = bf16[640,1024]{1,0:T(8,128)(2,1)} async-done(((bf16[2560,1024]{1,0:T(8,128)(2,1)}), bf16[640,1024]{1,0:T(8,128)(2,1)}) %reduce-scatter.4.cloned.1.call-update) | async-done | bytes 1310736
  560.7 2.4 copy.31
  563.2 9.0 %scatter_custom_fusion.4 = bf16[4096,640]{1,0:T(8,128)(2,1)} fusion(s32[1024]{0:T(1024)} %get-tuple-element.14, bf16[1024,640]{1,0:T(8,128)(2,1)} %copy.31, bf16[]{:T(256)} %constant.131.clone.1), kind=kCustom, calls=%fused_computation.24 | custom fusion | bytes 5243392 | tf_op jit(solution)/shard_map/scatter | solution.py:145
  (38 shorter events, 1.2 us)
Async XLA Ops:
  6.5 485.0 %copy-start = (bf16[640,2560]{1,0:T(8,128)(2,1)S(1)}, bf16[640,2560]{1,0:T(8,128)(2,1)}, u32[]{:S(2)}) copy-start(bf16[640,2560]{1,0:T(8,128)(2,1)} %param.7) | copy-start | bytes 9830404
  89.8 31.1 %all-to-all-start = ((bf16[32,32,640]{2,1,0:T(8,128)(2,1)}), bf16[32,32,640]{2,1,0:T(8,128)(2,1)}, u32[]{:S(2)}, u32[]{:S(2)}) async-start(bf16[32,32,640]{2,1,0:T(8,128)(2,1)} %bitcast.63), calls=%async_computation | async-start | bytes 2621440 | tf_op jit(solution)/shard_map/all_to_all | solution.py:47
  102.0 58.2 %all-gather.3.cloned.1.call-start = ((), (), s32[]{:S(2)}) async-start(), calls=%async_computation.4 | async-start | bytes 3276800 | tf_op jit(solution)/shard_map/all_gather | solution.py:23
  171.8 2.1 copy-start.1
  203.0 55.1 %all-to-all-start.1 = ((bf16[32,32,1920]{2,1,0:T(8,128)(2,1)}), bf16[32,32,1920]{2,1,0:T(8,128)(2,1)}, u32[]{:S(2)}, u32[]{:S(2)}) async-start(bf16[32,32,1920]{2,1,0:T(8,128)(2,1)} %bitcast.54), calls=%async_computation.1 | async-start | bytes 7864320 | tf_op jit(solution)/shard_map/all_to_all | solution.py:47
  284.3 121.0 %all-to-all-start.2 = ((bf16[4,1024,1280]{1,2,0:T(8,128)(2,1)}), bf16[4,1024,1280]{1,2,0:T(8,128)(2,1)}, u32[]{:S(2)}, u32[]{:S(2)}) async-start(bf16[4,1024,1280]{1,2,0:T(8,128)(2,1)} %stack.2), calls=%async_computation.2 | async-start | bytes 20971520 | tf_op jit(solution)/shard_map/all_to_all | solution.py:108
  290.3 270.4 %reduce-scatter.4.cloned.1.call-start = ((), (), s32[]{:S(2)}) async-start(), calls=%async_computation.5 | async-start | bytes 6553600
Sparse Core Ops, SparseCore 0:
  125.4 34.7 all-gather.2
  505.7 54.9 reduce-scatter.3
